TPU v7x, 256 devices: a whole 4x4x8 slice. The times are simulated.
256 devices in a mesh: leaf: 16 (over z, core), row: 4 (over y), col: 4 (over x).
Axes of the slice: x: 4, y: 4, z: 8, core: 2. Of those that a mesh axis runs over, the one named last changes fastest.
Arguments:
- rhs: bfloat16 [79360, 512], P(('leaf', 'row'), 'col'), may hold values from -6 to 6
- pivot_inverse: bfloat16 [79360, 2560], P('leaf', 'row'), may hold values from -0.125 to 0.125
- panel: bfloat16 [46080, 2560], P('leaf', 'row'), may hold values from -0.0625 to 0.0625
- live: int32 [31], replicated, may hold values from 10 to 20, as said below
- parent_map: int32 [30, 12], replicated, may hold values from 0 to 19, as said below
Outputs:
- forward_solution: bfloat16 [79360, 512], P(('leaf', 'row'), 'col')
- solution: bfloat16 [79360, 512], P(('leaf', 'row'), 'col')
Inputs may be any that keep to these rules, and one draw needn't show every extreme that they name: `live`: the root front (last index) is full, 20 blocks. `parent_map`: within one front's row the parent blocks are distinct.
All inputs are finite; a program needn't handle non-finite values.
Results may differ from a plain program's by a relative error of at most 0.012.
Values may be sent and summed in bfloat16 or wider, within the bound.
A program may use at most 64 MiB of HBM per device.

v0:
```python
import jax
import jax.numpy as jnp
from jax import lax
from jax.sharding import PartitionSpec as P

F = 2560
E = 1536


def cut_along(shard, dim, length):
    before, after = (shard.shape[:dim], shard.shape[dim + 1 :])
    return jnp.moveaxis(shard.reshape(*before, length, -1, *after), dim, 0)


def sum_at_owner(shard, axis, dim):
    tiles = cut_along(shard, dim, lax.axis_size(axis))
    arrived = lax.all_to_all(tiles, axis, split_axis=0, concat_axis=0, tiled=True)
    return arrived.astype(jnp.float32).sum(axis=0)


def from_partner(block, axis, apart):
    count = lax.axis_size(axis)
    route = []
    for low in range(count):
        high = low | 1 << apart
        if high != low and high < count:
            route += [(low, high), (high, low)]
    return lax.ppermute(block, axis, route)


def copy_for_each(shard, axis):
    length = lax.axis_size(axis)
    return lax.all_to_all(
        jnp.broadcast_to(shard[None], (length, *shard.shape)), axis, 0, 0, tiled=True
    )


def over_copies(shard, axis):
    return copy_for_each(shard, axis).sum(axis=0)


def in_order(tiles, dim):
    tiles = jnp.moveaxis(tiles, 0, dim)
    dims = tiles.shape
    return tiles.reshape(*dims[:dim], dims[dim] * dims[dim + 1], *dims[dim + 2 :])


def gather_directly(shard, axis, dim):
    return in_order(copy_for_each(shard, axis), dim)


def gather_packed(arrays, axis, dims):
    flat = jnp.concatenate([a.reshape(-1) for a in arrays])
    lines, at, finished = (lax.all_gather(flat, axis), 0, [])
    for a, dim in zip(arrays, dims):
        tiles = lines[:, at : at + a.size].reshape(-1, *a.shape)
        finished.append(in_order(tiles, dim))
        at += a.size
    return tuple(finished)


def doubling(stacked, bit_count, leaf_pos, swapper):
    for bit_no in range(bit_count):
        partner = swapper(stacked, bit_no)
        upper_half = jnp.right_shift(leaf_pos, bit_no) % 2 == 1
        stacked = jnp.where(
            upper_half,
            jnp.concatenate([partner, stacked], 0),
            jnp.concatenate([stacked, partner], 0),
        )
    return stacked


def halving(partial_value, bit_count, leaf_pos, swapper):
    for bit_no in reversed(range(bit_count)):
        halves = partial_value.reshape((2, partial_value.shape[0] // 2) + partial_value.shape[1:])
        upper_half = jnp.right_shift(leaf_pos, bit_no) % 2 == 1
        kept_half = jnp.where(upper_half, halves[1], halves[0])
        sent_half = jnp.where(upper_half, halves[0], halves[1])
        partial_value = kept_half + swapper(sent_half, bit_no)
    return partial_value[0]


def to_front(group_block, row_count):
    count_g, total_rows, row_width = group_block.shape
    piece_rows = total_rows // row_count
    return (
        group_block.reshape(count_g, row_count, piece_rows, row_width)
        .transpose(1, 0, 2, 3)
        .reshape(count_g * total_rows, row_width)
    )


def block_onehot(mapping):
    return (jnp.arange(F // 128, dtype=jnp.int32)[:, None] == mapping[None, :]).astype(jnp.bfloat16)


def pivot_sum(diag_block, quarter_rows):
    return sum_at_owner(
        jnp.dot(diag_block, quarter_rows, preferred_element_type=jnp.float32).astype(jnp.bfloat16),
        "row",
        0,
    )


def quarter_swap(values, bit_no):
    return from_partner(values, "leaf", bit_no)


def update_swap(values, bit_no):
    return from_partner(values, "leaf", bit_no)


def parent_swap(values, bit_no):
    return from_partner(values, "leaf", bit_no)


def reduce_swap(values, bit_no):
    return from_partner(values.astype(jnp.bfloat16), "leaf", bit_no).astype(values.dtype)


def on_device(rhs, pivot_inverse, panel, live, parent_map):
    leaves = lax.axis_size("leaf")
    row_count = lax.axis_size("row")
    tree_depth = leaves.bit_length() - 1
    leaf_pos = lax.axis_index("leaf")
    row_pos = lax.axis_index("row")
    columns = rhs.shape[1]
    quarter = F // row_count
    parent_blocks = F // 128
    child_blocks = E // 128
    layout = []
    vec_off, piv_off, pan_off, front_base = (0, 0, 0, 0)
    for level_no in range(tree_depth + 1):
        groups = 2**level_no
        layout.append((groups, vec_off, piv_off, pan_off, front_base))
        vec_off += F // (row_count * groups)
        piv_off += F // groups
        pan_off += E // groups
        front_base += leaves // groups
    forward_parts = []
    live_masks = []
    incoming = None
    for level_no in range(tree_depth + 1):
        groups, vec_off, piv_off, pan_off, front_base = layout[level_no]
        piece_rows = F // (row_count * groups)
        panel_rows = E // (row_count * groups)
        inner_pos = leaf_pos % groups
        front_no = jnp.right_shift(leaf_pos, level_no)
        live_rows = lax.dynamic_index_in_dim(live, front_base + front_no, 0, keepdims=False) * 128
        first_row = (row_pos * groups + inner_pos) * piece_rows
        live_mask = (first_row + jnp.arange(piece_rows, dtype=jnp.int32) < live_rows)[:, None]
        live_masks.append(live_mask)
        right_side = rhs[vec_off : vec_off + piece_rows]
        if incoming is not None:
            right_side = (right_side.astype(jnp.float32) - incoming).astype(jnp.bfloat16)
        masked = jnp.where(live_mask, right_side, jnp.zeros_like(right_side))
        quarter_rows = doubling(masked[None], level_no, leaf_pos, quarter_swap).reshape(
            quarter, columns
        )
        diag_block = pivot_inverse[piv_off : piv_off + F // groups]
        if level_no < tree_depth:
            off_block = panel[pan_off : pan_off + E // groups]
            forward_value = pivot_sum(diag_block, quarter_rows)
            update_rows = over_copies(
                jnp.dot(off_block, quarter_rows, preferred_element_type=jnp.float32), "row"
            ).astype(jnp.bfloat16)
        else:
            forward_value = pivot_sum(diag_block, quarter_rows)
        forward_parts.append(jnp.where(live_mask, forward_value, 0.0).astype(jnp.bfloat16))
        if level_no < tree_depth:
            gathered = doubling(update_rows[None], level_no + 1, leaf_pos, update_swap)
            parent_front = jnp.right_shift(leaf_pos, level_no + 1)
            assembled = jnp.zeros((parent_blocks, 128, columns), jnp.float32)
            for side_no in range(2):
                child_update = to_front(
                    gathered[side_no * groups : (side_no + 1) * groups], row_count
                )
                mapping = lax.dynamic_index_in_dim(
                    parent_map, front_base + 2 * parent_front + side_no, 0, keepdims=False
                )
                assembled = assembled + jnp.einsum(
                    "ke,eab->kab",
                    block_onehot(mapping),
                    child_update.reshape(child_blocks, 128, columns),
                    preferred_element_type=jnp.float32,
                )
            parent_groups = 2 * groups
            parent_rows = F // (row_count * parent_groups)
            parent_first = (row_pos * parent_groups + leaf_pos % parent_groups) * parent_rows
            incoming = lax.dynamic_slice_in_dim(
                assembled.reshape(F, columns), parent_first, parent_rows, 0
            )
    backward_parts = [None] * (tree_depth + 1)
    parent_value = None
    for level_no in reversed(range(tree_depth + 1)):
        groups, vec_off, piv_off, pan_off, front_base = layout[level_no]
        piece_rows = F // (row_count * groups)
        panel_rows = E // (row_count * groups)
        inner_pos = leaf_pos % groups
        front_no = jnp.right_shift(leaf_pos, level_no)
        diag_block = pivot_inverse[piv_off : piv_off + F // groups]
        own_piece = forward_parts[level_no]
        if level_no == tree_depth:
            own_rows = gather_directly(own_piece, "row", 0)
            partial_value = jnp.einsum(
                "ik,ia->ka", diag_block, own_rows, preferred_element_type=jnp.float32
            )
        else:
            own_rows, parent_gathered = gather_packed((own_piece, parent_value), "row", (0, 0))
            whole_parent = doubling(parent_gathered[None], level_no + 1, leaf_pos, parent_swap)
            parent_full = to_front(whole_parent, row_count)
            mapping = lax.dynamic_index_in_dim(parent_map, front_base + front_no, 0, keepdims=False)
            taken_rows = jnp.einsum(
                "ke,kab->eab",
                block_onehot(mapping),
                parent_full.reshape(parent_blocks, 128, columns),
                preferred_element_type=jnp.float32,
            ).astype(jnp.bfloat16)
            taken_rows = lax.dynamic_index_in_dim(
                taken_rows.reshape(row_count, groups, panel_rows, columns),
                inner_pos,
                1,
                keepdims=False,
            ).reshape(row_count * panel_rows, columns)
            off_block = panel[pan_off : pan_off + E // groups]
            partial_value = jnp.einsum(
                "ik,ia->ka", diag_block, own_rows, preferred_element_type=jnp.float32
            ) - jnp.einsum("ik,ia->ka", off_block, taken_rows, preferred_element_type=jnp.float32)
        if level_no == 0:
            reduced = partial_value
        else:
            reduced = halving(
                partial_value.reshape(groups, piece_rows, columns), level_no, leaf_pos, reduce_swap
            )
        parent_value = jnp.where(live_masks[level_no], reduced, 0.0).astype(jnp.bfloat16)
        backward_parts[level_no] = parent_value
    return (jnp.concatenate(forward_parts, 0), jnp.concatenate(backward_parts, 0))


def solution(mesh):
    in_specs = (P(("leaf", "row"), "col"), P("leaf", "row"), P("leaf", "row"), P(), P())
    out_specs = (P(("leaf", "row"), "col"), P(("leaf", "row"), "col"))
    return jax.shard_map(
        on_device, mesh=mesh, in_specs=in_specs, out_specs=out_specs, check_vma=False
    )
```

profile of v0, /device:TPU:1, one launch (start us, length us, event | category | flops | bytes accessed | tf_op | source)
XLA Modules:
  0.0 483.6 jit_solution(15990403695003136454)
XLA Ops:
  6.7 41.5 %all_to_all.50 = f32[4,1536,128]{2,1,0:T(8,128)S(1)} all-to-all(f32[4,1536,128]{2,1,0:T(8,128)S(1)} %broadcast_in_dim.224), channel_id=1, replica_groups=mesh['leaf'=16,'row'=4,'col'=4] {'row'}, dimensions={0} | all-to-all | bytes 6291456 | tf_op jit(solution)/shard_map/all_to_all | solution.py:33
  58.1 22.9 %all_to_all.51 = f32[4,768,128]{2,1,0:T(8,128)S(1)} all-to-all(f32[4,768,128]{2,1,0:T(8,128)S(1)} %broadcast_in_dim.229), channel_id=1, replica_groups=mesh['leaf'=16,'row'=4,'col'=4] {'row'}, dimensions={0} | all-to-all | bytes 3145728 | tf_op jit(solution)/shard_map/all_to_all | solution.py:33
  86.0 8.2 %collective-permute-done.3 = bf16[2,768,128]{2,1,0:T(8,128)(2,1)S(1)} collective-permute-done((bf16[2,768,128]{2,1,0:T(8,128)(2,1)S(1)}, bf16[2,768,128]{2,1,0:T(8,128)(2,1)S(1)}, u32[]{:S(2)}, u32[]{:S(2)}) %collective-permute-start.3) | collective-permute-done | bytes 393248 | tf_op jit(solution)/shard_map/ppermute | solution.py:28
  104.6 13.6 %all_to_all.52 = f32[4,384,128]{2,1,0:T(8,128)S(1)} all-to-all(f32[4,384,128]{2,1,0:T(8,128)S(1)} %broadcast_in_dim.234), channel_id=1, replica_groups=mesh['leaf'=16,'row'=4,'col'=4] {'row'}, dimensions={0} | all-to-all | bytes 1572864 | tf_op jit(solution)/shard_map/all_to_all | solution.py:33
  122.9 4.6 collective-permute-done.7
  127.6 3.5 collective-permute-start.8
  131.9 16.0 %collective-permute-done.8 = bf16[4,384,128]{2,1,0:T(8,128)(2,1)S(1)} collective-permute-done((bf16[4,384,128]{2,1,0:T(8,128)(2,1)S(1)}, bf16[4,384,128]{2,1,0:T(8,128)(2,1)S(1)}, u32[]{:S(2)}, u32[]{:S(2)}) %collective-permute-start.8) | collective-permute-done | bytes 393248 | tf_op jit(solution)/shard_map/ppermute | solution.py:28
  158.1 6.1 %collective-permute-done.11 = bf16[4,80,128]{1,2,0:T(8,128)(2,1)S(1)} collective-permute-done((bf16[4,80,128]{1,2,0:T(8,128)(2,1)S(1)}, bf16[4,80,128]{1,2,0:T(8,128)(2,1)S(1)}, u32[]{:S(2)}, u32[]{:S(2)}) %collective-permute-start.11) | collective-permute-done | bytes 81952 | tf_op jit(solution)/shard_map/ppermute | solution.py:28
  165.7 9.4 %all_to_all.53 = f32[4,192,128]{2,1,0:T(8,128)S(1)} all-to-all(f32[4,192,128]{2,1,0:T(8,128)S(1)} %broadcast_in_dim.239), channel_id=1, replica_groups=mesh['leaf'=16,'row'=4,'col'=4] {'row'}, dimensions={0} | all-to-all | bytes 786432 | tf_op jit(solution)/shard_map/all_to_all | solution.py:33
  185.0 8.7 %collective-permute-done.14 = bf16[4,192,128]{2,1,0:T(8,128)(2,1)S(1)} collective-permute-done((bf16[4,192,128]{2,1,0:T(8,128)(2,1)S(1)}, bf16[4,192,128]{2,1,0:T(8,128)(2,1)S(1)}, u32[]{:S(2)}, u32[]{:S(2)}) %collective-permute-start.14) | collective-permute-done | bytes 196640 | tf_op jit(solution)/shard_map/ppermute | solution.py:28
  193.7 7.1 %collective-permute-start.15 = (bf16[8,192,128]{2,1,0:T(8,128)(2,1)S(1)}, bf16[8,192,128]{2,1,0:T(8,128)(2,1)S(1)}, u32[]{:S(2)}, u32[]{:S(2)}) collective-permute-start(bf16[8,192,128]{2,1,0:T(8,128)(2,1)S(1)} %maximum_select_fusion.11), channel_id=1, source_target_pairs={{0,128},{128,0},{16,144},{144,16},{32,160},{160,32},{48,176},{176,... | collective-permute-start | bytes 1179656 | tf_op jit(solution)/shard_map/ppermute | solution.py:28
  201.6 16.7 %collective-permute-done.15 = bf16[8,192,128]{2,1,0:T(8,128)(2,1)S(1)} collective-permute-done((bf16[8,192,128]{2,1,0:T(8,128)(2,1)S(1)}, bf16[8,192,128]{2,1,0:T(8,128)(2,1)S(1)}, u32[]{:S(2)}, u32[]{:S(2)}) %collective-permute-start.15) | collective-permute-done | bytes 393248 | tf_op jit(solution)/shard_map/ppermute | solution.py:28
  231.6 4.8 collective-permute-done.19
  237.6 6.7 %all_to_all.54 = bf16[4,40,128]{2,1,0:T(8,128)(2,1)S(1)} all-to-all(bf16[4,40,128]{2,1,0:T(8,128)(2,1)S(1)} %bitcast.332), channel_id=1, replica_groups=mesh['leaf'=16,'row'=4,'col'=4] {'row'}, dimensions={0} | all-to-all | bytes 81920 | tf_op jit(solution)/shard_map/all_to_all | solution.py:17
  244.5 6.7 %all_to_all.55 = bf16[4,40,128]{2,1,0:T(8,128)(2,1)S(1)} all-to-all(bf16[4,40,128]{2,1,0:T(8,128)(2,1)S(1)} %broadcast_in_dim.251), channel_id=1, replica_groups=mesh['leaf'=16,'row'=4,'col'=4] {'row'}, dimensions={0} | all-to-all | bytes 81920 | tf_op jit(solution)/shard_map/all_to_all | solution.py:33
  255.4 9.4 %collective-permute-done.20 = bf16[8,40,128]{1,2,0:T(8,128)(2,1)S(1)} collective-permute-done((bf16[8,40,128]{1,2,0:T(8,128)(2,1)S(1)}, bf16[8,40,128]{1,2,0:T(8,128)(2,1)S(1)}, u32[]{:S(2)}, u32[]{:S(2)}) %collective-permute-start.20) | collective-permute-done | bytes 81952 | tf_op jit(solution)/shard_map/ppermute | solution.py:28
  267.5 3.3 all-to-all-start.6
  277.1 8.2 %collective-permute-start.23 = (bf16[1,40,128]{1,2,0:T(8,128)(2,1)S(1)}, bf16[1,40,128]{1,2,0:T(8,128)(2,1)S(1)}, u32[]{:S(2)}, u32[]{:S(2)}) collective-permute-start(bf16[1,40,128]{1,2,0:T(8,128)(2,1)S(1)} %select_convert_fusion.12), channel_id=1, source_target_pairs={{0,16},{16,0},{32,48},{48,32},{64,80},{80,64},{96,112},{112,96},{1... | collective-permute-start | bytes 30728 | tf_op jit(solution)/shard_map/ppermute | solution.py:28
  286.3 9.2 %all-gather = bf16[61440]{0:T(1024)(128)(2,1)S(1)} all-gather(bf16[15360]{0:T(1024)(128)(2,1)S(1)} %pad_maximum_fusion.3), channel_id=2, replica_groups=mesh['leaf'=16,'row'=4,'col'=4] {'row'}, dimensions={0}, use_global_device_ids=true | all-gather | bytes 153600 | tf_op jit(solution)/shard_map/all_gather | solution.py:54
  302.4 3.3 all-to-all-start.4
  310.2 10.3 %collective-permute-done.26 = bf16[4,160,128]{1,2,0:T(8,128)(2,1)S(1)} collective-permute-done((bf16[4,160,128]{1,2,0:T(8,128)(2,1)S(1)}, bf16[4,160,128]{1,2,0:T(8,128)(2,1)S(1)}, u32[]{:S(2)}, u32[]{:S(2)}) %collective-permute-start.26) | collective-permute-done | bytes 163872 | tf_op jit(solution)/shard_map/ppermute | solution.py:28
  320.7 3.3 collective-permute-start.27
  324.4 25.2 %collective-permute-done.27 = bf16[8,160,128]{1,2,0:T(8,128)(2,1)S(1)} collective-permute-done((bf16[8,160,128]{1,2,0:T(8,128)(2,1)S(1)}, bf16[8,160,128]{1,2,0:T(8,128)(2,1)S(1)}, u32[]{:S(2)}, u32[]{:S(2)}) %collective-permute-start.27) | collective-permute-done | bytes 327712 | tf_op jit(solution)/shard_map/ppermute | solution.py:28
  352.4 8.8 %collective-permute-done.28 = bf16[4,80,128]{1,2,0:T(8,128)(2,1)S(1)} collective-permute-done((bf16[4,80,128]{1,2,0:T(8,128)(2,1)S(1)}, bf16[4,80,128]{1,2,0:T(8,128)(2,1)S(1)}, u32[]{:S(2)}, u32[]{:S(2)}) %collective-permute-start.28) | collective-permute-done | bytes 81952 | tf_op jit(solution)/shard_map/ppermute | solution.py:28
  367.4 9.9 %all-gather.1 = bf16[122880]{0:T(1024)(128)(2,1)S(1)} all-gather(bf16[30720]{0:T(1024)(128)(2,1)S(1)} %pad_maximum_fusion.2), channel_id=3, replica_groups=mesh['leaf'=16,'row'=4,'col'=4] {'row'}, dimensions={0}, use_global_device_ids=true | all-gather | bytes 307200 | tf_op jit(solution)/shard_map/all_gather | solution.py:54
  383.4 3.6 all-to-all-start.2
  394.2 3.5 all-to-all-start
  400.4 17.8 %collective-permute-done.33 = bf16[4,320,128]{1,2,0:T(8,128)(2,1)S(1)} collective-permute-done((bf16[4,320,128]{1,2,0:T(8,128)(2,1)S(1)}, bf16[4,320,128]{1,2,0:T(8,128)(2,1)S(1)}, u32[]{:S(2)}, u32[]{:S(2)}) %collective-permute-start.33) | collective-permute-done | bytes 327712 | tf_op jit(solution)/shard_map/ppermute | solution.py:28
  421.2 4.4 collective-permute-done.34
  428.2 11.3 %all-gather.2 = bf16[245760]{0:T(1024)(128)(2,1)S(1)} all-gather(bf16[61440]{0:T(1024)(128)(2,1)S(1)} %pad_maximum_fusion.1), channel_id=4, replica_groups=mesh['leaf'=16,'row'=4,'col'=4] {'row'}, dimensions={0}, use_global_device_ids=true | all-gather | bytes 614400 | tf_op jit(solution)/shard_map/all_gather | solution.py:54
  444.2 8.2 %collective-permute-done.37 = bf16[2,640,128]{2,1,0:T(8,128)(2,1)S(1)} collective-permute-done((bf16[2,640,128]{2,1,0:T(8,128)(2,1)S(1)}, bf16[2,640,128]{2,1,0:T(8,128)(2,1)S(1)}, u32[]{:S(2)}, u32[]{:S(2)}) %collective-permute-start.37) | collective-permute-done | bytes 327712 | tf_op jit(solution)/shard_map/ppermute | solution.py:28
  459.6 13.4 %all-gather.3 = bf16[491520]{0:T(1024)(128)(2,1)S(1)} all-gather(bf16[122880]{0:T(1024)(128)(2,1)S(1)} %pad_maximum_fusion), channel_id=5, replica_groups=mesh['leaf'=16,'row'=4,'col'=4] {'row'}, dimensions={0}, use_global_device_ids=true | all-gather | bytes 1228800 | tf_op jit(solution)/shard_map/all_gather | solution.py:54
  (314 shorter events, 147.9 us)
Async XLA Ops:
  48.4 4.4 collective-permute-start
  83.5 10.8 %collective-permute-start.3 = (bf16[2,768,128]{2,1,0:T(8,128)(2,1)S(1)}, bf16[2,768,128]{2,1,0:T(8,128)(2,1)S(1)}, u32[]{:S(2)}, u32[]{:S(2)}) collective-permute-start(bf16[2,768,128]{2,1,0:T(8,128)(2,1)S(1)} %maximum_select_fusion.9), channel_id=1, source_target_pairs={{0,32},{32,0},{16,48},{48,16},{64,96},{96,64},{80,112},{112,80},{1... | collective-permute-start | bytes 1179656 | tf_op jit(solution)/shard_map/ppermute | solution.py:28
  98.0 4.8 collective-permute-start.5
  121.3 6.2 %collective-permute-start.7 = (bf16[2,384,128]{2,1,0:T(8,128)(2,1)S(1)}, bf16[2,384,128]{2,1,0:T(8,128)(2,1)S(1)}, u32[]{:S(2)}, u32[]{:S(2)}) collective-permute-start(bf16[2,384,128]{2,1,0:T(8,128)(2,1)S(1)} %maximum_select_fusion.21), channel_id=1, source_target_pairs={{0,32},{32,0},{16,48},{48,16},{64,96},{96,64},{80,112},{112,80},{1... | collective-permute-start | bytes 589832 | tf_op jit(solution)/shard_map/ppermute | solution.py:28
  127.6 20.4 %collective-permute-start.8 = (bf16[4,384,128]{2,1,0:T(8,128)(2,1)S(1)}, bf16[4,384,128]{2,1,0:T(8,128)(2,1)S(1)}, u32[]{:S(2)}, u32[]{:S(2)}) collective-permute-start(bf16[4,384,128]{2,1,0:T(8,128)(2,1)S(1)} %maximum_select_fusion.10), channel_id=1, source_target_pairs={{0,64},{64,0},{16,80},{80,16},{32,96},{96,32},{48,112},{112,48},{1... | collective-permute-start | bytes 1179656 | tf_op jit(solution)/shard_map/ppermute | solution.py:28
  152.3 3.2 collective-permute-start.10
  155.5 8.7 %collective-permute-start.11 = (bf16[4,80,128]{1,2,0:T(8,128)(2,1)S(1)}, bf16[4,80,128]{1,2,0:T(8,128)(2,1)S(1)}, u32[]{:S(2)}, u32[]{:S(2)}) collective-permute-start(bf16[4,80,128]{1,2,0:T(8,128)(2,1)S(1)} %maximum_select_fusion.28), channel_id=1, source_target_pairs={{0,64},{64,0},{16,80},{80,16},{32,96},{96,32},{48,112},{112,48},{1... | collective-permute-start | bytes 245768 | tf_op jit(solution)/shard_map/ppermute | solution.py:28
  178.1 4.1 collective-permute-start.13
  182.2 11.5 %collective-permute-start.14 = (bf16[4,192,128]{2,1,0:T(8,128)(2,1)S(1)}, bf16[4,192,128]{2,1,0:T(8,128)(2,1)S(1)}, u32[]{:S(2)}, u32[]{:S(2)}) collective-permute-start(bf16[4,192,128]{2,1,0:T(8,128)(2,1)S(1)} %maximum_select_fusion.22), channel_id=1, source_target_pairs={{0,64},{64,0},{16,80},{80,16},{32,96},{96,32},{48,112},{112,48},{1... | collective-permute-start | bytes 589832 | tf_op jit(solution)/shard_map/ppermute | solution.py:28
  193.7 24.6 %collective-permute-start.15 = (bf16[8,192,128]{2,1,0:T(8,128)(2,1)S(1)}, bf16[8,192,128]{2,1,0:T(8,128)(2,1)S(1)}, u32[]{:S(2)}, u32[]{:S(2)}) collective-permute-start(bf16[8,192,128]{2,1,0:T(8,128)(2,1)S(1)} %maximum_select_fusion.11), channel_id=1, source_target_pairs={{0,128},{128,0},{16,144},{144,16},{32,160},{160,32},{48,176},{176,... | collective-permute-start | bytes 1179656 | tf_op jit(solution)/shard_map/ppermute | solution.py:28
  224.8 4.3 collective-permute-start.18
  229.1 7.3 %collective-permute-start.19 = (bf16[8,40,128]{2,1,0:T(8,128)(2,1)S(1)}, bf16[8,40,128]{2,1,0:T(8,128)(2,1)S(1)}, u32[]{:S(2)}, u32[]{:S(2)}) collective-permute-start(bf16[8,40,128]{2,1,0:T(8,128)(2,1)S(1)} %maximum_select_fusion.31), channel_id=1, source_target_pairs={{0,128},{128,0},{16,144},{144,16},{32,160},{160,32},{48,176},{176,... | collective-permute-start | bytes 245768 | tf_op jit(solution)/shard_map/ppermute | solution.py:28
  252.7 12.1 %collective-permute-start.20 = (bf16[8,40,128]{1,2,0:T(8,128)(2,1)S(1)}, bf16[8,40,128]{1,2,0:T(8,128)(2,1)S(1)}, u32[]{:S(2)}, u32[]{:S(2)}) collective-permute-start(bf16[8,40,128]{1,2,0:T(8,128)(2,1)S(1)} %copy.525), channel_id=1, source_target_pairs={{0,128},{128,0},{16,144},{144,16},{32,160},{160,32},{48,176},{176,... | collective-permute-start | bytes 245768 | tf_op jit(solution)/shard_map/ppermute | solution.py:28
  264.9 8.7 %collective-permute-start.21 = (bf16[4,40,128]{1,2,0:T(8,128)(2,1)S(1)}, bf16[4,40,128]{1,2,0:T(8,128)(2,1)S(1)}, u32[]{:S(2)}, u32[]{:S(2)}) collective-permute-start(bf16[4,40,128]{1,2,0:T(8,128)(2,1)S(1)} %select_convert_fusion.1), channel_id=1, source_target_pairs={{0,64},{64,0},{16,80},{80,16},{32,96},{96,32},{48,112},{112,48},{1... | collective-permute-start | bytes 122888 | tf_op jit(solution)/shard_map/ppermute | solution.py:28
  267.5 7.8 %all-to-all-start.6 = ((bf16[4,80,128]{2,1,0:T(8,128)(2,1)}), bf16[4,80,128]{2,1,0:T(8,128)(2,1)S(1)}, u32[]{:S(2)}, u32[]{:S(2)}) async-start(bf16[4,80,128]{2,1,0:T(8,128)(2,1)} %bitcast.45), calls=%async_computation.6 | async-start | bytes 163840 | tf_op jit(solution)/shard_map/all_to_all | solution.py:17
  273.6 3.4 collective-permute-start.22
  277.1 9.1 %collective-permute-start.23 = (bf16[1,40,128]{1,2,0:T(8,128)(2,1)S(1)}, bf16[1,40,128]{1,2,0:T(8,128)(2,1)S(1)}, u32[]{:S(2)}, u32[]{:S(2)}) collective-permute-start(bf16[1,40,128]{1,2,0:T(8,128)(2,1)S(1)} %select_convert_fusion.12), channel_id=1, source_target_pairs={{0,16},{16,0},{32,48},{48,32},{64,80},{80,64},{96,112},{112,96},{1... | collective-permute-start | bytes 30728 | tf_op jit(solution)/shard_map/ppermute | solution.py:28
  295.8 4.1 collective-permute-start.24
  299.9 5.9 %collective-permute-start.25 = (bf16[2,160,128]{1,2,0:T(8,128)(2,1)S(1)}, bf16[2,160,128]{1,2,0:T(8,128)(2,1)S(1)}, u32[]{:S(2)}, u32[]{:S(2)}) collective-permute-start(bf16[2,160,128]{1,2,0:T(8,128)(2,1)S(1)} %maximum_select_fusion.29), channel_id=1, source_target_pairs={{0,32},{32,0},{16,48},{48,16},{64,96},{96,64},{80,112},{112,80},{1... | collective-permute-start | bytes 245768 | tf_op jit(solution)/shard_map/ppermute | solution.py:28
  302.4 59.0 %all-to-all-start.4 = ((bf16[4,160,128]{2,1,0:T(8,128)(2,1)}), bf16[4,160,128]{2,1,0:T(8,128)(2,1)S(1)}, u32[]{:S(2)}, u32[]{:S(2)}) async-start(bf16[4,160,128]{2,1,0:T(8,128)(2,1)} %bitcast.29), calls=%async_computation.4 | async-start | bytes 327680 | tf_op jit(solution)/shard_map/all_to_all | solution.py:17
  306.0 14.5 %collective-permute-start.26 = (bf16[4,160,128]{1,2,0:T(8,128)(2,1)S(1)}, bf16[4,160,128]{1,2,0:T(8,128)(2,1)S(1)}, u32[]{:S(2)}, u32[]{:S(2)}) collective-permute-start(bf16[4,160,128]{1,2,0:T(8,128)(2,1)S(1)} %maximum_select_fusion.19), channel_id=1, source_target_pairs={{0,64},{64,0},{16,80},{80,16},{32,96},{96,32},{48,112},{112,48},{1... | collective-permute-start | bytes 491528 | tf_op jit(solution)/shard_map/ppermute | solution.py:28
  320.7 28.9 %collective-permute-start.27 = (bf16[8,160,128]{1,2,0:T(8,128)(2,1)S(1)}, bf16[8,160,128]{1,2,0:T(8,128)(2,1)S(1)}, u32[]{:S(2)}, u32[]{:S(2)}) collective-permute-start(bf16[8,160,128]{1,2,0:T(8,128)(2,1)S(1)} %maximum_select_fusion.8), channel_id=1, source_target_pairs={{0,128},{128,0},{16,144},{144,16},{32,160},{160,32},{48,176},{176,... | collective-permute-start | bytes 983048 | tf_op jit(solution)/shard_map/ppermute | solution.py:28
  352.2 9.1 %collective-permute-start.28 = (bf16[4,80,128]{1,2,0:T(8,128)(2,1)S(1)}, bf16[4,80,128]{1,2,0:T(8,128)(2,1)S(1)}, u32[]{:S(2)}, u32[]{:S(2)}) collective-permute-start(bf16[4,80,128]{1,2,0:T(8,128)(2,1)S(1)} %copy.540), channel_id=1, source_target_pairs={{0,64},{64,0},{16,80},{80,16},{32,96},{96,32},{48,112},{112,48},{1... | collective-permute-start | bytes 245768 | tf_op jit(solution)/shard_map/ppermute | solution.py:28
  377.7 9.3 %collective-permute-start.31 = (bf16[1,320,128]{1,2,0:T(8,128)(2,1)S(1)}, bf16[1,320,128]{1,2,0:T(8,128)(2,1)S(1)}, u32[]{:S(2)}, u32[]{:S(2)}) collective-permute-start(bf16[1,320,128]{1,2,0:T(8,128)(2,1)S(1)} %copy.543), channel_id=1, source_target_pairs={{0,16},{16,0},{32,48},{48,32},{64,80},{80,64},{96,112},{112,96},{1... | collective-permute-start | bytes 245768 | tf_op jit(solution)/shard_map/ppermute | solution.py:28
  383.4 10.8 %all-to-all-start.2 = ((bf16[4,320,128]{2,1,0:T(8,128)(2,1)}), bf16[4,320,128]{2,1,0:T(8,128)(2,1)S(1)}, u32[]{:S(2)}, u32[]{:S(2)}) async-start(bf16[4,320,128]{2,1,0:T(8,128)(2,1)} %bitcast.13), calls=%async_computation.2 | async-start | bytes 655360 | tf_op jit(solution)/shard_map/all_to_all | solution.py:17
  387.1 10.9 %collective-permute-start.32 = (bf16[2,320,128]{1,2,0:T(8,128)(2,1)S(1)}, bf16[2,320,128]{1,2,0:T(8,128)(2,1)S(1)}, u32[]{:S(2)}, u32[]{:S(2)}) collective-permute-start(bf16[2,320,128]{1,2,0:T(8,128)(2,1)S(1)} %maximum_select_fusion.23), channel_id=1, source_target_pairs={{0,32},{32,0},{16,48},{48,16},{64,96},{96,64},{80,112},{112,80},{1... | collective-permute-start | bytes 491528 | tf_op jit(solution)/shard_map/ppermute | solution.py:28
  394.2 49.4 %all-to-all-start = ((bf16[4,640,128]{1,2,0:T(8,128)(2,1)}), bf16[4,640,128]{1,2,0:T(8,128)(2,1)S(1)}, u32[]{:S(2)}, u32[]{:S(2)}) async-start(bf16[4,640,128]{1,2,0:T(8,128)(2,1)} %bitcast.263), calls=%async_computation | async-start | bytes 1310720 | tf_op jit(solution)/shard_map/all_to_all | solution.py:17
  398.1 20.1 %collective-permute-start.33 = (bf16[4,320,128]{1,2,0:T(8,128)(2,1)S(1)}, bf16[4,320,128]{1,2,0:T(8,128)(2,1)S(1)}, u32[]{:S(2)}, u32[]{:S(2)}) collective-permute-start(bf16[4,320,128]{1,2,0:T(8,128)(2,1)S(1)} %maximum_select_fusion.12), channel_id=1, source_target_pairs={{0,64},{64,0},{16,80},{80,16},{32,96},{96,32},{48,112},{112,48},{1... | collective-permute-start | bytes 983048 | tf_op jit(solution)/shard_map/ppermute | solution.py:28
  420.9 4.7 collective-permute-start.34
  440.0 3.4 collective-permute-start.36
  443.5 9.0 %collective-permute-start.37 = (bf16[2,640,128]{2,1,0:T(8,128)(2,1)S(1)}, bf16[2,640,128]{2,1,0:T(8,128)(2,1)S(1)}, u32[]{:S(2)}, u32[]{:S(2)}) collective-permute-start(bf16[2,640,128]{2,1,0:T(8,128)(2,1)S(1)} %maximum_select_fusion.15), channel_id=1, source_target_pairs={{0,32},{32,0},{16,48},{48,16},{64,96},{96,64},{80,112},{112,80},{1... | collective-permute-start | bytes 983048 | tf_op jit(solution)/shard_map/ppermute | solution.py:28
  474.2 6.6 %collective-permute-start.39 = (bf16[1,1280,128]{2,1,0:T(8,128)(2,1)S(1)}, bf16[1,1280,128]{2,1,0:T(8,128)(2,1)S(1)}, u32[]{:S(2)}, u32[]{:S(2)}) collective-permute-start(bf16[1,1280,128]{2,1,0:T(8,128)(2,1)S(1)} %broadcast_in_dim_reshape_reshape.15), channel_id=1, source_target_pairs={{0,16},{16,0},{32,48},{48,32},{64,80},{80,64},{96,112},{112,96},{1... | collective-permute-start | bytes 983048 | tf_op jit(solution)/shard_map/ppermute | solution.py:28
  (21 other events, 203.6 us)
where the time goes:
time: 493 us; the launch traced here: 484 us
  waiting for transfers between devices  187 us (38%)
  blocking collectives  145 us (29%)
  starting transfers between devices  85.2 us (17%)
  matrix products  36.1 us (7%)
  local copies, waits for them, and re-layouts  20.3 us (4%)
  between operations  5.84 us (1%)
    ppermute x40, waiting for transfers between devices, from_partner(): return lax.ppermute(block, axis, route)  183 us
    all_to_all x5, blocking collectives, copy_for_each(): lax.all_to_all(jnp.broadcast_to(shard[None], (length, *shard.shape)), axi...  94.1 us
    ppermute x40, starting transfers between devices, from_partner(): return lax.ppermute(block, axis, route)  71.4 us
    all_gather x4, blocking collectives, gather_packed(): lines, at, finished = (lax.all_gather(flat, axis), 0, [])  43.9 us
    all_to_all x4, starting transfers between devices, sum_at_owner(): lax.all_to_all(tiles, axis, split_axis=0, concat_axis=0, tiled=True)  13.7 us
  transfers between devices with their start and end apart: 44, of which 37 were waited for; matrix products, arithmetic and copies ran while one was open for 6% of the time, Pallas kernels for 0%

commit v1 on v0

v1 whole, which is shorter than its diff:
```python
import jax
import jax.numpy as jnp
from jax import lax
from jax.experimental import pallas as pl
from jax.experimental.pallas import tpu as pltpu
from jax.sharding import PartitionSpec as P

MESH = pl.DeviceIdType.MESH
F32 = jnp.float32
BF16 = jnp.bfloat16

F = 2560
E = 1536
ROWS = 4
TOP = 4
Q = F // ROWS
H = Q // 2
EB = E // 128
C = 128

GROUPS = [2**k for k in range(TOP + 1)]
VOFF = [0, 640, 960, 1120, 1200]
DOFF = [0, 2560, 3840, 4480, 4800]
WOFF = [0, 1536, 2304, 2688]
BASE = [0, 16, 24, 28, 30]


def pad16(n):
    return (n + 15) // 16 * 16


def scratch_shapes():
    shapes = {}
    for k in range(TOP + 1):
        g = GROUPS[k]
        shapes[f"d{k}"] = ((F // g, Q), BF16)
        shapes[f"x{k}"] = ((Q, C), BF16)
        shapes[f"dty{k}"] = ((Q, C), F32)
        shapes[f"v{k}"] = ((F // g, C), BF16)
        shapes[f"vr{k}"] = ((3, Q // g if k < TOP else F // g, C), BF16)
        shapes[f"y{k}"] = ((F // g, C), BF16)
        if 0 < k < TOP:
            shapes[f"b{k}"] = ((Q, C), BF16)
        if k < TOP:
            shapes[f"w{k}"] = ((E // g, Q), BF16)
            shapes[f"u{k}"] = ((E // g, C), BF16)
            shapes[f"p{k}"] = ((F, C), BF16)
            shapes[f"pr{k}"] = ((ROWS, H, C), BF16)
            shapes[f"ys{k}"] = ((ROWS, H, C), BF16)
            shapes[f"yr{k}"] = ((3, H, C), BF16)
            shapes[f"c{k}"] = ((2, H, C), BF16)
            shapes[f"t{k}"] = ((E // g, C), BF16)
        if k > 0:
            shapes[f"bp{k}"] = ((2, H, C), BF16)
            shapes[f"bpr{k}"] = ((H, C), BF16)
            shapes[f"s{k}"] = ((F, C), BF16)
    for name, n in (("f1", 2), ("f2", 4), ("f3", 8), ("r4", 8), ("r3", 4), ("r2", 2)):
        if n == 2:
            shapes[f"zs_{name}"] = ((H, C), BF16)
            shapes[f"zr_{name}"] = ((H, C), BF16)
        else:
            pch = pad16(H // n)
            shapes[f"zs_{name}"] = ((n, pch, C), BF16)
            shapes[f"zr_{name}"] = ((n - 1, pch, C), BF16)
            shapes[f"zg_{name}"] = ((n, pch, C), BF16)
    shapes["b4s"] = ((16, 48, C), BF16)
    shapes["b4"] = ((Q, C), F32)
    shapes["half"] = ((H, C), F32)
    shapes["acc"] = ((Q, C), F32)
    shapes["fin"] = ((F // 16, C), F32)
    return shapes


SHAPES = scratch_shapes()
NAMES = list(SHAPES)
N_REMOTE = 200
N_LOCAL = 9


def kernel(rhs, piv, pan, live, pmap, fwd, sol, *refs):
    S = dict(zip(NAMES, refs))
    send_sem, recv_sem, load_sem = refs[len(NAMES) :]
    leaf = lax.axis_index("leaf")
    row = lax.axis_index("row")
    par = leaf % 2
    chip = leaf // 2
    counter = [0]
    unsent = []

    def xor(a, m):
        return a + m - 2 * (a & m)

    def send(src, dst, device):
        i = counter[0]
        counter[0] += 1
        copy = pltpu.make_async_remote_copy(
            src_ref=src,
            dst_ref=dst,
            send_sem=send_sem.at[i],
            recv_sem=recv_sem.at[i],
            device_id=device,
            device_id_type=MESH,
        )
        copy.start()
        unsent.append(copy)
        return copy

    def to_leaf(src, dst, m):
        return send(src, dst, {"leaf": xor(leaf, m)})

    def to_row(src, dst, m):
        return send(src, dst, {"row": xor(row, m)})

    loads = {}
    order = [("w0", pan, 0), ("d0", piv, 0), ("w1", pan, 1), ("d1", piv, 1), ("w2", pan, 2), ("d2", piv, 2)]
    order += [("w3", pan, 3), ("d3", piv, 3), ("d4", piv, 4)]
    for n, (name, ref, k) in enumerate(order):
        rows = S[name].shape[0]
        off = (WOFF if ref is pan else DOFF)[k]
        copy = pltpu.make_async_copy(ref.at[pl.ds(off, rows)], S[name], load_sem.at[n])
        copy.start()
        loads[name] = copy

    barrier = pltpu.get_barrier_semaphore()
    for m in range(1, 16):
        pl.semaphore_signal(barrier, inc=1, device_id={"leaf": xor(leaf, m)}, device_id_type=MESH)
    for m in range(1, ROWS):
        pl.semaphore_signal(barrier, inc=1, device_id={"row": xor(row, m)}, device_id_type=MESH)

    def live_rows(k):
        return live[BASE[k] + leaf // GROUPS[k]] * 128

    def below(n, start, k):
        return (lax.broadcasted_iota(jnp.int32, (n, C), 0) + start) < live_rows(k)

    def targets(k):
        g = GROUPS[k]
        t = leaf % g
        child = BASE[k] + leaf // g
        found = {}
        for r in range(ROWS):
            for j in range(3):
                block = pmap[child, 3 * r + (3 * t + j) // g]
                found[r, j] = jnp.full((16, C), block.astype(F32), F32).astype(BF16)
        return found

    def place(k):
        g = GROUPS[k]
        n = 128 // g
        u, p = S[f"u{k}"], S[f"p{k}"]
        found = targets(k)
        groups = [range(3)] if g == 1 else [[0], [1], [2]]

        def body(i, carry):
            for js in groups:
                at = ((3 * (leaf % g) + js[0]) % g) * n + i * 16
                vals = {
                    (r, j): u[pl.ds(pl.multiple_of((3 * r + j) * n + i * 16, 16), 16), :]
                    for r in range(ROWS)
                    for j in js
                }
                for b in range(F // 128):
                    where = pl.ds(pl.multiple_of(b * 128 + at, 16), 16)
                    out = p[where, :] if g == 2 else jnp.zeros((16, C), BF16)
                    for key, val in vals.items():
                        out = jnp.where(found[key] == BF16(b), val, out)
                    p[where, :] = out
            return carry

        lax.fori_loop(0, n // 16, body, 0)

    def pick(k):
        g = GROUPS[k]
        n = 128 // g
        s, w = S[f"s{k + 1}"], S[f"t{k}"]
        found = targets(k)

        def body(i, carry):
            for js in [range(3)] if g == 1 else [[0], [1], [2]]:
                at = ((3 * (leaf % g) + js[0]) % g) * n + i * 16
                keys = [(r, j) for r in range(ROWS) for j in js]
                outs = {key: jnp.zeros((16, C), BF16) for key in keys}
                for b in range(F // 128):
                    val = s[pl.ds(pl.multiple_of(b * 128 + at, 16), 16), :]
                    for key in keys:
                        outs[key] = jnp.where(found[key] == BF16(b), val, outs[key])
                for r, j in keys:
                    w[pl.ds(pl.multiple_of((3 * r + j) * n + i * 16, 16), 16), :] = outs[r, j]
            return carry

        lax.fori_loop(0, n // 16, body, 0)

    def product(dst, mat, x, chunk):
        rows = mat.shape[0]
        chunk = min(chunk, rows)
        val = x[...]
        if chunk == rows:
            dst[pl.ds(0, rows), :] = jnp.dot(mat[...], val, preferred_element_type=F32).astype(BF16)
            return

        def body(i, carry):
            at = pl.multiple_of(i * chunk, chunk)
            dst[pl.ds(at, chunk), :] = jnp.dot(
                mat[pl.ds(at, chunk), :], val, preferred_element_type=F32
            ).astype(BF16)
            return carry

        lax.fori_loop(0, rows // chunk, body, 0)

    def transposed(dst, mat, x, less=None):
        def body(i, carry):
            at = pl.multiple_of(i * 128, 128)
            out = lax.dot_general(
                mat[:, pl.ds(at, 128)], x[...], (((0,), (0,)), ((), ())), preferred_element_type=F32
            )
            if less is not None:
                out = less[pl.ds(at, 128), :] - out
            dst[pl.ds(at, 128), :] = out
            return carry

        lax.fori_loop(0, Q // 128, body, 0)

    def chip_sum(name, n, half):
        if n == 1:
            return
        zs, zr = S[f"zs_{name}"], S[f"zr_{name}"]
        if n == 2:
            zs[...] = half[...].astype(BF16)
            copy = to_leaf(zs, zr, 2)
            copy.wait_recv()
            half[...] = zs[...].astype(F32) + zr[...].astype(F32)
            return
        zg = S[f"zg_{name}"]
        ch = H // n
        mine = chip % n
        for j in range(n):
            zs[j, 0:ch, :] = half[j * ch : (j + 1) * ch, :].astype(BF16)
        copies = [to_leaf(zs.at[xor(mine, m)], zr.at[m - 1], 2 * m) for m in range(1, n)]
        total = zs[mine].astype(F32)
        for m in range(1, n):
            copies[m - 1].wait_recv()
            total = total + zr[m - 1].astype(F32)
        zg[mine] = total.astype(BF16)
        copies = [to_leaf(zg.at[mine], zg.at[mine], 2 * m) for m in range(1, n)]
        for copy in copies:
            copy.wait_recv()
        for j in range(n):
            half[j * ch : (j + 1) * ch, :] = zg[j, 0:ch, :].astype(F32)

    v_copies = {}
    y_copies = {}

    def send_v(k):
        h = Q // GROUPS[k]
        v_copies[k] = [
            to_row(S[f"v{k}"].at[pl.ds(pl.multiple_of(xor(row, m) * h, h), h)], S[f"vr{k}"].at[m - 1], m)
            for m in range(1, ROWS)
        ]

    def finish_v(k):
        g = GROUPS[k]
        h = Q // g
        at = pl.multiple_of(row * h, h)
        total = S[f"v{k}"][pl.ds(at, h), :].astype(F32)
        for m in range(1, ROWS):
            v_copies[k][m - 1].wait_recv()
            total = total + S[f"vr{k}"][m - 1].astype(F32)
        piece = jnp.where(below(h, (row * g + leaf % g) * h, k), total, 0.0).astype(BF16)
        fwd[VOFF[k] : VOFF[k] + h, :] = piece
        y = S[f"y{k}"]
        y[pl.ds(at, h), :] = piece
        y_copies[k] = [to_row(y.at[pl.ds(at, h)], y.at[pl.ds(at, h)], m) for m in range(1, ROWS)]

    def finish_y(k):
        for copy in y_copies[k]:
            copy.wait_recv()
        transposed(S[f"dty{k}"], S[f"d{k}"], S[f"y{k}"])

    for k in range(1, TOP):
        S[f"p{k}"][...] = jnp.zeros((F, C), BF16)
    S["x0"][...] = jnp.where(below(Q, row * Q, 0), rhs[0:Q, :], jnp.zeros((Q, C), BF16))

    b_copies = {}
    for k in range(1, TOP):
        h = Q // GROUPS[k]
        S[f"b{k}"][pl.ds(pl.multiple_of((leaf % GROUPS[k]) * h, h), h), :] = rhs[VOFF[k] : VOFF[k] + h, :]
    S["b4s"][leaf, 0:40, :] = rhs[1200:1240, :]
    S["b4s"][leaf, 32:48, :] = jnp.concatenate([rhs[1232:1240, :], jnp.zeros((8, C), BF16)], 0)

    pl.semaphore_wait(barrier, 18)

    for k in range(1, TOP):
        g = GROUPS[k]
        h = Q // g
        mine = pl.ds(pl.multiple_of((leaf % g) * h, h), h)
        b_copies[k] = [to_leaf(S[f"b{k}"].at[mine], S[f"b{k}"].at[mine], m) for m in range(1, g)]
    b_copies[4] = [to_leaf(S["b4s"].at[leaf], S["b4s"].at[leaf], m) for m in range(1, 16)]

    for k in range(TOP):
        g = GROUPS[k]
        u, p, pr, ys, yr, c = (S[f"{name}{k}"] for name in ("u", "p", "pr", "ys", "yr", "c"))
        loads[f"w{k}"].wait()
        product(u, S[f"w{k}"], S[f"x{k}"], 384)
        place(k)
        pairs = [
            to_leaf(p.at[pl.ds(pl.multiple_of(r * Q + (1 - par) * H, 16), H)], pr.at[r], 1) for r in range(ROWS)
        ]
        loads[f"d{k}"].wait()
        product(S[f"v{k}"], S[f"d{k}"], S[f"x{k}"], 640)
        for r in range(ROWS):
            pairs[r].wait_recv()
            own = p[pl.ds(pl.multiple_of(r * Q + par * H, 16), H), :]
            ys[r] = (own.astype(F32) + pr[r].astype(F32)).astype(BF16)
        copies = [to_row(ys.at[xor(row, m)], yr.at[m - 1], m) for m in range(1, ROWS)]
        send_v(k)
        if k >= 1:
            finish_v(k - 1)
        if k >= 2:
            finish_y(k - 2)
        for copy in b_copies[k + 1]:
            copy.wait_recv()
        if k + 1 == TOP:
            for j in range(16):
                S["b4"][40 * j : 40 * j + 40, :] = S["b4s"][j, 0:40, :].astype(F32)
        total = ys[row].astype(F32)
        for m in range(1, ROWS):
            copies[m - 1].wait_recv()
            total = total + yr[m - 1].astype(F32)
        half = S["half"]
        half[...] = total
        chip_sum(f"f{k}", g, half)
        c[par] = half[...].astype(BF16)
        pair = to_leaf(c.at[par], c.at[par], 1)
        pair.wait_recv()
        b = S[f"b{k + 1}"]
        for s in range(2):
            x = b[s * H : (s + 1) * H, :].astype(F32) - c[s].astype(F32)
            x = jnp.where(below(H, row * Q + s * H, k + 1), x, 0.0)
            S[f"x{k + 1}"][s * H : (s + 1) * H, :] = x.astype(BF16)

    loads["d4"].wait()
    n = F // 16
    v = S["v4"]
    product(v, S["d4"], S["x4"], n)
    copies = [to_row(v, S["vr4"].at[m - 1], m) for m in range(1, ROWS)]
    finish_v(3)
    finish_y(2)
    total = v[...].astype(F32)
    for m in range(1, ROWS):
        copies[m - 1].wait_recv()
        total = total + S["vr4"][m - 1].astype(F32)
    S["fin"][...] = total
    for r in range(ROWS):
        at = (r * 16 + leaf) * 40
        S["fin"][r * 40 : r * 40 + 40, :] = jnp.where(below(40, at, 4), S["fin"][r * 40 : r * 40 + 40, :], 0.0)
    S["y4"][...] = S["fin"][...].astype(BF16)
    fwd[1200:1240, :] = S["fin"][pl.ds(pl.multiple_of(row * 40, 8), 40), :].astype(BF16)
    acc = S["acc"]
    transposed(acc, S["d4"], S["y4"])

    for k in range(TOP, 0, -1):
        g = GROUPS[k]
        h = Q // g
        if k < TOP:
            pick(k)
            transposed(acc, S[f"w{k}"], S[f"t{k}"], S[f"dty{k}"])
        bp, bpr, s = S[f"bp{k}"], S[f"bpr{k}"], S[f"s{k}"]
        for i in range(2):
            bp[i] = acc[i * H : (i + 1) * H, :].astype(BF16)
        pair = to_leaf(bp.at[1 - par], bpr, 1)
        if k == TOP:
            finish_y(3)
        pair.wait_recv()
        half = S["half"]
        half[...] = acc[pl.ds(pl.multiple_of(par * H, H), H), :] + bpr[...].astype(F32)
        chip_sum(f"r{k}", g // 2, half)
        def part(r, i):
            return s.at[pl.ds(pl.multiple_of(r * Q + i * H, 16), H)]

        own = part(row, par)
        own[...] = jnp.where(below(H, row * Q + par * H, k), half[...], 0.0).astype(BF16)
        copies = [to_row(own, own, m) for m in range(1, ROWS)]
        pairs = [to_leaf(own, own, 1)]
        for m in range(1, ROWS):
            copies[m - 1].wait_recv()
            block = part(xor(row, m), par)
            pairs.append(to_leaf(block, block, 1))
        for copy in pairs:
            copy.wait_recv()
        if k == TOP:
            acc[...] = s[pl.ds(pl.multiple_of(row * Q, 16), Q), :].astype(F32)
            sol[1200:1240, :] = acc[pl.ds(pl.multiple_of(leaf * 40, 8), 40), :].astype(BF16)
        else:
            sol[VOFF[k] : VOFF[k] + h, :] = s[pl.ds(pl.multiple_of(row * Q + (leaf % g) * h, 16), h), :]
    pick(0)
    transposed(acc, S["w0"], S["t0"], S["dty0"])
    sol[0:Q, :] = jnp.where(below(Q, row * Q, 0), acc[...], 0.0).astype(BF16)

    for copy in unsent:
        copy.wait_send()


def on_device(rhs, pivot_inverse, panel, live, parent_map):
    shape = jax.ShapeDtypeStruct(rhs.shape, BF16)
    vmem = pl.BlockSpec(memory_space=pltpu.VMEM)
    smem = pl.BlockSpec(memory_space=pltpu.SMEM)
    hbm = pl.BlockSpec(memory_space=pl.ANY)
    return pl.pallas_call(
        kernel,
        out_shape=(shape, shape),
        in_specs=[vmem, hbm, hbm, smem, smem],
        out_specs=(vmem, vmem),
        scratch_shapes=[pltpu.VMEM(*SHAPES[name]) for name in NAMES]
        + [
            pltpu.SemaphoreType.DMA((N_REMOTE,)),
            pltpu.SemaphoreType.DMA((N_REMOTE,)),
            pltpu.SemaphoreType.DMA((N_LOCAL,)),
        ],
        compiler_params=pltpu.CompilerParams(collective_id=0, has_side_effects=True),
    )(rhs, pivot_inverse, panel, live, parent_map)


def solution(mesh):
    in_specs = (P(("leaf", "row"), "col"), P("leaf", "row"), P("leaf", "row"), P(), P())
    out_specs = (P(("leaf", "row"), "col"), P(("leaf", "row"), "col"))
    return jax.shard_map(
        on_device, mesh=mesh, in_specs=in_specs, out_specs=out_specs, check_vma=False
    )
```

time: 493 us -> 151 us (0.31); the launches traced: 484 us -> 151 us
  waiting for transfers between devices: 187 us -> 0 us
  Pallas kernels: 0 us -> 145 us
  blocking collectives: 145 us -> 0 us
  starting transfers between devices: 85.2 us -> 0 us
  matrix products: 36.1 us -> 0 us
  local copies, waits for them, and re-layouts: 20.3 us -> 4.81 us
  between operations: 5.84 us -> 0.64 us
    ppermute x40 -> x0, waiting for transfers between devices: 183 us -> none  [from_partner(): return lax.ppermute(block, axis, route)]
    pallas_call x0 -> x1, Pallas kernels: none -> 145 us  [on_device(): pl.pallas_call(kernel, out_shape=(shape, shape), in_specs=[vmem, hbm, hbm...]
    all_to_all x6 -> x0, blocking collectives: 101 us -> none  [the longest x5 94.1 us: copy_for_each(): lax.all_to_all(jnp.broadcast_to(shard[None], (length, *shard.shape)), axi...]
    ppermute x40 -> x0, starting transfers between devices: 71.4 us -> none  [from_partner(): return lax.ppermute(block, axis, route)]
    all_gather x4 -> x0, blocking collectives: 43.9 us -> none  [gather_packed(): lines, at, finished = (lax.all_gather(flat, axis), 0, [])]
    dot_general x30 -> x0, matrix products: 36.1 us -> none  [the longest x5 9.69 us: pivot_sum(): jnp.dot(diag_block, quarter_rows, preferred_element_type=jnp.float32)]
    all_to_all x4 -> x0, starting transfers between devices: 13.7 us -> none  [sum_at_owner(): lax.all_to_all(tiles, axis, split_axis=0, concat_axis=0, tiled=True)]
  transfers between devices with their start and end apart: 44 -> 0, of which waited for: 37 -> 0; matrix products, arithmetic and copies ran while one was open for 6% -> 0% of each run, Pallas kernels for 0% -> 0%
where the time goes in v1:
time: 151 us
  Pallas kernels  145 us (96%)
  local copies, waits for them, and re-layouts  4.81 us (3%)
    pallas_call x1, Pallas kernels, on_device(): pl.pallas_call(kernel, out_shape=(shape, shape), in_specs=[vmem, hbm, hbm...  145 us
    unnamed x3, local copies, waits for them, and re-layouts  4.81 us

profile of v1, /device:TPU:1, one launch (start us, length us, event | category | flops | bytes accessed | tf_op | source)
XLA Modules:
  0.0 150.8 jit_solution(11187142739193468863)
XLA Ops:
  0.6 1.4 copy.7.pmap
  2.0 145.4 %shard_map.68 = (bf16[1240,128]{1,0:T(8,128)(2,1)}, bf16[1240,128]{1,0:T(8,128)(2,1)}) custom-call(bf16[1240,128]{1,0:T(8,128)(2,1)} %rhs.1, bf16[4960,640]{1,0:T(8,128)(2,1)} %piv.1, bf16[2880,640]{1,0:T(8,128)(2,1)} %pan.1, s32[31]{0:T(128)} %live.1, s32[30,12]{1,0:T(8,128)} %copy.7.pmap), custom_call_target="tpu_custom_call" | custom-call | tf_op jit(solution)/shard_map/pallas_call | solution.py:408
  147.4 1.7 %copy.10 = bf16[1240,128]{1,0:T(8,128)(2,1)} copy(bf16[1240,128]{1,0:T(8,128)(2,1)} %get-tuple-element.4) | data formatting | bytes 634880
  149.1 1.7 %copy.11 = bf16[1240,128]{1,0:T(8,128)(2,1)} copy(bf16[1240,128]{1,0:T(8,128)(2,1)} %get-tuple-element.5) | data formatting | bytes 634880
